TPU v7x, 128 devices: a whole 4x4x4 slice. The times are simulated.
128 devices in a mesh: chan: 32 (over x, y, core), int: 4 (over z).
Axes of the slice: x: 4, y: 4, z: 4, core: 2. Of those that a mesh axis runs over, the one named last changes fastest.
Arguments:
- t_pp: bfloat16 [131072, 2048], P(('chan', 'int')), may hold values from -6 to 6
- interaction: bfloat16 [4, 2048, 2048], P(None, None, 'int'), may hold values from -0.125 to 0.125
- send_order: int32 [131072], P(('chan', 'int')), may hold values from 0 to 1023, as said below
- recv_order: int32 [131072], P(('chan', 'int')), may hold values from 0 to 1023, as said below
- ph_channel: int32 [131072], P('chan'), may hold values from 0 to 4, as said below
- recouple_weight: float32 [131072], P('chan'), may hold values from -1.5 to 1.5
Outputs:
- term_pp: bfloat16 [131072, 2048], P(('chan', 'int'))
Inputs may be any that keep to these rules, and one draw needn't show every extreme that they name: `send_order`: within each device's 1024 slots a permutation of its local rows. `recv_order`: within each device's 1024 slots a permutation of its received rows. `ph_channel`: non-decreasing within each device's 1024 slots; the value 4 marks empty slots, which come last; some device has no empty slot.
All inputs are finite; a program needn't handle non-finite values.
Results may differ from a plain program's by a relative error of at most 0.001.
Values may be sent and summed in bfloat16 or wider, within the bound.
A program may use at most 128 MiB of HBM per device.

v0:
```python
import jax
import jax.numpy as jnp
from jax import lax
from jax.sharding import PartitionSpec as P


def channel_counts(channel_ids, channels):
    table = channel_ids[:, None] == jnp.arange(channels, dtype=jnp.int32)[None, :]
    return jnp.sum(table.astype(jnp.int32), axis=0)


def finish(product, channel_ids, scale, channels):
    live = (channel_ids < channels)[:, None]
    return jnp.where(live, scale[:, None] * product, jnp.float32(0.0)).astype(jnp.bfloat16)


def on_device(t_pp, interaction, send_order, recv_order, ph_channel, recouple_weight):
    slot_count = t_pp.shape[0]
    channels = interaction.shape[0]
    outgoing = jnp.take(t_pp, send_order, axis=0)
    arrived = lax.all_to_all(outgoing, "chan", split_axis=0, concat_axis=0, tiled=True)
    ph_rows = jnp.take(arrived, recv_order, axis=0)
    group_size = lax.axis_size("int")
    everyone = lax.all_gather(ph_rows, "int", axis=0, tiled=True)
    shares = []
    for member in range(group_size):
        member_ids = ph_channel[member * slot_count : (member + 1) * slot_count]
        member_scale = recouple_weight[member * slot_count : (member + 1) * slot_count]
        member_rows = everyone[member * slot_count : (member + 1) * slot_count]
        product = lax.ragged_dot(
            member_rows,
            interaction,
            channel_counts(member_ids, channels),
            preferred_element_type=jnp.float32,
        )
        shares.append(finish(product, member_ids, member_scale, channels))
    column_shares = jnp.concatenate(shares, axis=0)
    z_ph = lax.all_to_all(column_shares, "int", split_axis=0, concat_axis=1, tiled=True)
    back_rows = jnp.zeros_like(z_ph).at[recv_order].set(z_ph)
    returned = lax.all_to_all(back_rows, "chan", split_axis=0, concat_axis=0, tiled=True)
    return jnp.zeros_like(returned).at[send_order].set(returned)


def solution(mesh):
    in_specs = (
        P(("chan", "int"), None),
        P(None, None, "int"),
        P(("chan", "int")),
        P(("chan", "int")),
        P("chan"),
        P("chan"),
    )
    out_specs = P(("chan", "int"), None)
    return jax.shard_map(
        on_device, mesh=mesh, in_specs=in_specs, out_specs=out_specs, check_vma=False
    )
```

profile of v0, /device:TPU:1, one launch (start us, length us, event | category | flops | bytes accessed | tf_op | source)
XLA Modules:
  0.0 458.6 jit_solution(18042309666216540853)
XLA Ops:
  6.5 0.7 broadcast_clamp_fusion.1
  7.2 0.7 compare_and_fusion.1
  7.9 11.5 %gather_fusion = bf16[1024,2048]{1,0:T(8,128)(2,1)} fusion(bf16[1024,2048]{1,0:T(8,128)(2,1)} %param.8, s32[1024]{0:T(1024)S(1)} %get-tuple-element.40), kind=kCustom, calls=%fused_computation.clone | custom fusion | bytes 8392704 | tf_op jit(solution)/shard_map/jit(_take)/gather | solution.py:20
  19.5 4.6 %broadcast_select_fusion.1 = bf16[1024,2048]{1,0:T(8,128)(2,1)} fusion(bf16[1024,2048]{1,0:T(8,128)(2,1)} %gather_fusion, pred[1024]{0:T(1024)(128)(4,1)S(1)} %compare_and_fusion.1), kind=kLoop, calls=%fused_computation.6 | loop fusion | flops 2097152 | bytes 8389632 | tf_op jit(solution)/shard_map/jit(_take)/select_n | solution.py:20
  24.1 8.8 %all-to-all-start = ((bf16[32,32,2048]{2,1,0:T(8,128)(2,1)}), bf16[32,32,2048]{2,1,0:T(8,128)(2,1)}, u32[]{:S(2)}, u32[]{:S(2)}) async-start(bf16[32,32,2048]{2,1,0:T(8,128)(2,1)} %bitcast.8), calls=%async_computation | async-start | bytes 8388608 | tf_op jit(solution)/shard_map/all_to_all | solution.py:21
  32.9 0.0 all-gather.2.cloned.1.call-start
  33.0 52.0 %all-to-all-done = bf16[32,32,2048]{2,1,0:T(8,128)(2,1)} async-done(((bf16[32,32,2048]{2,1,0:T(8,128)(2,1)}), bf16[32,32,2048]{2,1,0:T(8,128)(2,1)}, u32[]{:S(2)}, u32[]{:S(2)}) %all-to-all-start) | async-done | bytes 4194336 | tf_op jit(solution)/shard_map/all_to_all | solution.py:21
  85.0 11.5 %gather_fusion.1 = bf16[1024,2048]{1,0:T(8,128)(2,1)} fusion(bf16[1024,2048]{1,0:T(8,128)(2,1)} %bitcast.1, s32[1024]{0:T(1024)S(1)} %get-tuple-element.38), kind=kCustom, calls=%fused_computation.1.clone | custom fusion | bytes 8392704 | tf_op jit(solution)/shard_map/jit(_take)/gather | solution.py:22
  96.5 4.6 %broadcast_select_fusion = bf16[1024,2048]{1,0:T(8,128)(2,1)} fusion(bf16[1024,2048]{1,0:T(8,128)(2,1)} %gather_fusion.1, pred[1024]{0:T(1024)(128)(4,1)S(1)} %compare_and_fusion), kind=kLoop, calls=%fused_computation.5 | loop fusion | flops 2097152 | bytes 8389632 | tf_op jit(solution)/shard_map/jit(_take)/select_n | solution.py:22
  101.2 0.7 copy-done
  101.9 0.7 convert_reduce_fusion
  102.6 1.4 ragged-dot-metadata
  104.0 1.4 ragged-dot-metadata.1
  105.4 0.7 convert_reduce_fusion.2
  106.1 1.4 ragged-dot-metadata.2
  107.5 1.4 ragged-dot-metadata.3
  108.9 148.0 %all-gather.2.cloned.1.call-done = bf16[4096,2048]{1,0:T(8,128)(2,1)} async-done(((bf16[1024,2048]{1,0:T(8,128)(2,1)}), bf16[4096,2048]{1,0:T(8,128)(2,1)}) %all-gather.2.cloned.1.call-update) | async-done | bytes 16777232 | tf_op jit(solution)/shard_map/all_gather | solution.py:24
  256.9 12.4 %fusion.4 = (bf16[1024,2048]{1,0:T(8,128)(2,1)}, bf16[1024,2048]{1,0:T(8,128)(2,1)}, bf16[1024,2048]{1,0:T(8,128)(2,1)}, bf16[1024,2048]{1,0:T(8,128)(2,1)}) fusion(bf16[4096,2048]{1,0:T(8,128)(2,1)} %all-gather.2.cloned.1.call-done), kind=kLoop, calls=%fused_computation.33 | loop fusion | bytes 33554432 | tf_op jit(solution)/shard_map/slice | solution.py:29
  269.4 11.1 %ragged-dot-none = f32[1024,512]{1,0:T(8,128)} custom-call(s32[1]{0:T(128)} %get-tuple-element.6, s32[5]{0:T(128)} %get-tuple-element.7, s32[7]{0:T(128)} %get-tuple-element.8, s32[7]{0:T(128)} %get-tuple-element.9, s32[1]{0:T(128)} %get-tuple-element.6, bf16[1024,2048]{1,0:T(8,128)(2,1)} %get-tuple-element.23, bf16[4,2048,512]{2,1,0:T(8,128)(2,1)} %param.9), custom_call_target="tpu_custom_call" | custom-call | flops 2147483648 | bytes 14680080 | tf_op jit(solution)/shard_map/ragged_dot_general/ragged-dot-none
  280.5 1.9 select_convert_fusion
  282.4 11.1 %ragged-dot-none.1 = f32[1024,512]{1,0:T(8,128)} custom-call(s32[1]{0:T(128)} %get-tuple-element.10, s32[5]{0:T(128)} %get-tuple-element.11, s32[7]{0:T(128)} %get-tuple-element.12, s32[7]{0:T(128)} %get-tuple-element.13, s32[1]{0:T(128)} %get-tuple-element.10, bf16[1024,2048]{1,0:T(8,128)(2,1)} %get-tuple-element.24, bf16[4,2048,512]{2,1,0:T(8,128)(2,1)} %param.9), custom_call_target="tpu_custom_call" | custom-call | flops 2147483648 | bytes 14680080 | tf_op jit(solution)/shard_map/ragged_dot_general/ragged-dot-none
  293.5 1.9 select_convert_fusion.1
  295.4 10.8 %ragged-dot-none.2 = f32[1024,512]{1,0:T(8,128)} custom-call(s32[1]{0:T(128)} %get-tuple-element.14, s32[5]{0:T(128)} %get-tuple-element.15, s32[7]{0:T(128)} %get-tuple-element.16, s32[7]{0:T(128)} %get-tuple-element.17, s32[1]{0:T(128)} %get-tuple-element.14, bf16[1024,2048]{1,0:T(8,128)(2,1)} %get-tuple-element.25, bf16[4,2048,512]{2,1,0:T(8,128)(2,1)} %param.9), custom_call_target="tpu_custom_call" | custom-call | flops 2147483648 | bytes 14680080 | tf_op jit(solution)/shard_map/ragged_dot_general/ragged-dot-none
  306.2 1.9 select_convert_fusion.2
  308.2 11.9 %ragged-dot-none.3 = f32[1024,512]{1,0:T(8,128)} custom-call(s32[1]{0:T(128)} %get-tuple-element.18, s32[5]{0:T(128)} %get-tuple-element.19, s32[7]{0:T(128)} %get-tuple-element.20, s32[7]{0:T(128)} %get-tuple-element.21, s32[1]{0:T(128)} %get-tuple-element.18, bf16[1024,2048]{1,0:T(8,128)(2,1)} %get-tuple-element.22, bf16[4,2048,512]{2,1,0:T(8,128)(2,1)} %param.9), custom_call_target="tpu_custom_call" | custom-call | flops 2147483648 | bytes 14680080 | tf_op jit(solution)/shard_map/ragged_dot_general/ragged-dot-none
  320.0 1.9 select_convert_fusion.3
  322.0 0.3 pad_maximum_fusion
  322.3 42.3 %all_to_all.43 = bf16[4,1024,512]{2,1,0:T(8,128)(2,1)S(1)} all-to-all(bf16[4,1024,512]{2,1,0:T(8,128)(2,1)S(1)} %bitcast.9), channel_id=1, replica_groups=mesh['chan'=32,'int'=4] {'int'}, dimensions={0} | all-to-all | bytes 8388608 | tf_op jit(solution)/shard_map/all_to_all | solution.py:38
  364.6 2.7 copy.10
  367.2 10.0 %scatter_custom_fusion = bf16[1024,2048]{1,0:T(8,128)(2,1)} fusion(s32[1024]{0:T(1024)S(1)} %get-tuple-element.39, bf16[1024,2048]{1,0:T(8,128)(2,1)} %bitcast.13, bf16[]{:T(256)} %constant.0.clone.1), kind=kCustom, calls=%fused_computation.13 | custom fusion | bytes 4194816 | tf_op jit(solution)/shard_map/scatter | solution.py:39
  377.3 64.4 %all_to_all.44 = bf16[32,32,2048]{2,1,0:T(8,128)(2,1)} all-to-all(bf16[32,32,2048]{2,1,0:T(8,128)(2,1)} %bitcast.10), channel_id=1, replica_groups=mesh['chan'=32,'int'=4] {'chan'}, dimensions={0} | all-to-all | bytes 8388608 | tf_op jit(solution)/shard_map/all_to_all | solution.py:40
  441.6 10.1 %scatter_custom_fusion.1 = bf16[1024,2048]{1,0:T(8,128)(2,1)} fusion(s32[1024]{0:T(1024)S(1)} %get-tuple-element.41, bf16[1024,2048]{1,0:T(8,128)(2,1)} %bitcast.12, bf16[]{:T(256)} %constant.0.clone.1), kind=kCustom, calls=%fused_computation.11 | custom fusion | bytes 4194816 | tf_op jit(solution)/shard_map/scatter | solution.py:41
  (11 shorter events, 0.1 us)
Async XLA Ops:
  24.1 8.8 %copy-start.1 = (s32[1024]{0:T(1024)S(1)}, s32[1024]{0:T(1024)}, u32[]{:S(2)}) copy-start(s32[1024]{0:T(1024)} %param.11) | copy-start | bytes 12292
  24.1 60.9 %all-to-all-start = ((bf16[32,32,2048]{2,1,0:T(8,128)(2,1)}), bf16[32,32,2048]{2,1,0:T(8,128)(2,1)}, u32[]{:S(2)}, u32[]{:S(2)}) async-start(bf16[32,32,2048]{2,1,0:T(8,128)(2,1)} %bitcast.8), calls=%async_computation | async-start | bytes 8388608 | tf_op jit(solution)/shard_map/all_to_all | solution.py:21
  32.9 224.1 %all-gather.2.cloned.1.call-start = ((), (), s32[]{:S(2)}) async-start(), calls=%async_computation.3 | async-start | bytes 20971520 | tf_op jit(solution)/shard_map/all_gather | solution.py:24
  101.2 0.7 copy-start
  101.2 7.7 %copy-start.2 = (f32[4096]{0:T(1024)S(1)}, f32[4096]{0:T(1024)}, u32[]{:S(2)}) copy-start(f32[4096]{0:T(1024)} %param.13) | copy-start | bytes 49156
Sparse Core Ops, SparseCore 0:
  101.3 155.5 all-gather.1
where the time goes:
time: 460 us; the launch traced here: 459 us
  waiting for transfers between devices  200 us (43%)
  blocking collectives  107 us (23%)
  local copies, waits for them, and re-layouts  59 us (13%)
  Pallas kernels  50.3 us (11%)
  other arithmetic  20.2 us (4%)
  between operations  13.5 us (3%)
  starting transfers between devices  8.8 us (2%)
    all_gather x1, waiting for transfers between devices, on_device(): everyone = lax.all_gather(ph_rows, 'int', axis=0, tiled=True)  148 us
    all_to_all x1, blocking collectives, on_device(): lax.all_to_all(back_rows, 'chan', split_axis=0, concat_axis=0, tiled=True)  64.4 us
    all_to_all x1, waiting for transfers between devices, on_device(): lax.all_to_all(outgoing, 'chan', split_axis=0, concat_axis=0, tiled=True)  52 us
    another operation x4, Pallas kernels  44.9 us
    all_to_all x1, blocking collectives, on_device(): lax.all_to_all(column_shares, 'int', split_axis=0, concat_axis=1, tiled=T...  42.3 us
    slice x1, local copies, waits for them, and re-layouts, on_device(): member_rows = everyone[member * slot_count:(member + 1) * slot_count]  12.4 us
    gather x1, local copies, waits for them, and re-layouts, on_device(): ph_rows = jnp.take(arrived, recv_order, axis=0)  11.5 us
    gather x1, local copies, waits for them, and re-layouts, on_device(): outgoing = jnp.take(t_pp, send_order, axis=0)  11.5 us
  transfers between devices with their start and end apart: 2, of which 2 were waited for; matrix products, arithmetic and copies ran while one was open for 0% of the time, Pallas kernels for 1%

commit v1 on v0

v1 whole, which is shorter than its diff:
```python
import jax
import jax.numpy as jnp
from jax import lax
from jax.experimental import pallas as pl
from jax.experimental.pallas import tpu as pltpu
from jax.sharding import PartitionSpec as P

NX, NY, NCORE, NZ = 4, 4, 2, 4
G = 4
MT = 512
BF = jnp.bfloat16
F32 = jnp.float32


def spread(position, values):
    hit = position[None, :] == jnp.arange(position.shape[0], dtype=jnp.int32)[:, None]
    return [jnp.sum(jnp.where(hit, v[None, :], jnp.float32(0.0)), axis=1) for v in values]


def kernel(t_hbm, w_hbm, ch_ref, scale_ref, out_hbm, wbuf, tm, tbuf, acc, local_sem, out_sem, send_sem, recv_sem):
    rows, width = t_hbm.shape
    chan = lax.axis_index("chan")
    z = lax.axis_index("int")
    core = chan % NCORE
    y = (chan // NCORE) % NY
    x = chan // (NCORE * NY)

    def at_xy(px, py, pc):
        return {"chan": (px * NY + py) * NCORE + pc}

    xp, xm = at_xy((x + 1) % NX, y, core), at_xy((x + NX - 1) % NX, y, core)
    yp, ym = at_xy(x, (y + 1) % NY, core), at_xy(x, (y + NY - 1) % NY, core)
    zp, zm = {"int": (z + 1) % NZ}, {"int": (z + NZ - 1) % NZ}
    sib = at_xy(x, y, 1 - core)
    links = (xp, xm, yp, ym, zp, zm, sib)
    XP, XM, YP, YM, ZP, ZM, SIB = range(7)
    steps = 3 * G

    t_copy = pltpu.make_async_copy(t_hbm, tbuf, local_sem.at[G])
    t_copy.start()
    for g in range(G):
        for c in range(4):
            pltpu.make_async_copy(w_hbm.at[c, :, g], wbuf.at[pl.ds(g * 16 + c * 4, 4)], local_sem.at[g]).start()

    barrier = pltpu.get_barrier_semaphore()
    for peer in links:
        pl.semaphore_signal(barrier, inc=1, device_id=peer, device_id_type=pl.DeviceIdType.MESH)
    pl.semaphore_wait(barrier, 7)

    def spot(dq, g, c, kq):
        return ((dq * G + g) * 4 + c) * 4 + kq

    def send(link, src, dst_index):
        pltpu.make_async_remote_copy(
            src_ref=src,
            dst_ref=wbuf.at[dst_index],
            send_sem=send_sem.at[link],
            recv_sem=recv_sem.at[dst_index - G * 16],
            device_id=links[link],
            device_id_type=pl.DeviceIdType.MESH,
        ).start()

    def forward(link, index):
        send(link, wbuf.at[index], index)

    def arrive(index):
        pltpu.make_async_copy(wbuf.at[index], wbuf.at[index], recv_sem.at[index - G * 16]).wait()

    cx, cy = 2 * core, 2 * core + 1

    for g in range(G):
        for c, kq in ((cx, x), (cy, y)):
            src = w_hbm.at[c, kq, g]
            send(ZP, src, spot(3, g, c, kq))
            send(ZM, src, spot(1, g, c, kq))

    t_copy.wait()
    for c in range(4):
        @pl.loop(0, rows // 128)
        def _(m):
            r = pl.multiple_of(m * 128, 128)
            keep = (ch_ref[pl.ds(r, 128), :] == jnp.float32(c))
            for g in range(G):
                for kq in range(4):
                    col = (kq * G + g) * 128
                    v = tbuf[pl.ds(r, 128), col : col + 128]
                    tm[g, pl.ds(r, 128), (c * 4 + kq) * 128 : (c * 4 + kq + 1) * 128] = jnp.where(
                        keep, v.astype(F32), jnp.float32(0.0)
                    ).astype(BF)

    def place(s):
        early = 1 - s // (2 * G)
        dq = early * (1 + 2 * (s % 2)) + (1 - early) * 2
        g = early * (s // 2) + (1 - early) * (s - 2 * G)
        return dq, g

    def unit(dq, g, slot):
        @pl.loop(0, rows // MT)
        def _(m):
            r = pl.ds(pl.multiple_of(m * MT, MT), MT)

            @pl.when(g == 0)
            def _():
                acc[slot, r, :] = jnp.zeros((MT, 512), F32)

            rhs = wbuf[pl.ds((dq * G + g) * 16, 16)].reshape(2048, 512)
            acc[slot, r, :] += jnp.dot(tm[g, r, :], rhs, preferred_element_type=F32)

        @pl.when(g == G - 1)
        def _():
            col = pl.ds(pl.multiple_of(((z + dq) % NZ) * 512, 512), 512)

            @pl.loop(0, rows // 128)
            def _(m):
                r = pl.ds(pl.multiple_of(m * 128, 128), 128)
                sc = scale_ref[r, :]
                for part in range(4):
                    lanes = pl.ds(pl.multiple_of(((z + dq) % NZ) * 512 + part * 128, 128), 128)
                    tbuf[r, lanes] = (acc[slot, r, part * 128 : (part + 1) * 128] * sc).astype(BF)

            pltpu.make_async_copy(tbuf.at[:, col], out_hbm.at[:, col], out_sem.at[dq]).start()

    def step(s, carry):
        @pl.when(s < steps)
        def _():
            dq, g = place(s)
            for c, kq, plus, minus in ((cx, x, XP, XM), (cy, y, YP, YM)):
                index = spot(dq, g, c, kq)
                arrive(index)
                forward(plus, index)
                forward(minus, index)
                forward(SIB, index)

            @pl.when(dq == 3)
            def _():
                send(ZP, wbuf.at[spot(3, g, cx, x)], spot(2, g, cx, x))

            @pl.when(dq == 1)
            def _():
                send(ZM, wbuf.at[spot(1, g, cy, y)], spot(2, g, cy, y))

        @pl.when(jnp.logical_and(s >= 1, s < steps + 1))
        def _():
            dq, g = place(s - 1)
            for c, kq, plus, minus in ((cx, x, XP, XM), (cy, y, YP, YM)):
                below, above = spot(dq, g, c, (kq + 3) % 4), spot(dq, g, c, (kq + 1) % 4)
                arrive(below)
                arrive(above)

                @pl.when(g < G // 2)
                def _():
                    forward(plus, below)

                @pl.when(g >= G // 2)
                def _():
                    forward(minus, above)

                forward(SIB, below)
                forward(SIB, above)

        @pl.when(s < G)
        def _():
            pltpu.make_async_copy(wbuf.at[pl.ds(s * 16, 16)], wbuf.at[pl.ds(s * 16, 16)], local_sem.at[s]).wait()
            unit(0, s, 1)

        @pl.when(s >= 3)
        def _():
            dq, g = place(s - 3)
            for c in (2 - 2 * core, 3 - 2 * core):
                for kq in range(4):
                    arrive(spot(dq, g, c, kq))
            unit(dq, g, dq - 1)

        @pl.when(jnp.logical_and(s >= 2, s < steps + 2))
        def _():
            dq, g = place(s - 2)
            for c, kq in ((cx, x), (cy, y)):
                index = spot(dq, g, c, (kq + 2) % 4)
                arrive(index)
                forward(SIB, index)

        return carry

    lax.fori_loop(0, steps + 3, step, 0)

    for link, count in ((XP, 18), (XM, 18), (YP, 18), (YM, 18), (ZP, 12), (ZM, 12), (SIB, 96)):
        whole = wbuf.at[pl.ds(0, count)]
        pltpu.make_async_copy(whole, whole, send_sem.at[link]).wait()
    for dq in range(4):
        part = pl.ds(0, 512)
        pltpu.make_async_copy(tbuf.at[:, part], out_hbm.at[:, part], out_sem.at[dq]).wait()


def on_device(t_pp, interaction, send_order, recv_order, ph_channel, recouple_weight):
    rows = t_pp.shape[0]
    n_chan = lax.axis_size("chan")
    quota = rows // n_chan
    start = lax.axis_index("int") * rows
    ids = lax.dynamic_slice(ph_channel, (start,), (rows,)).astype(F32)
    scale = lax.dynamic_slice(recouple_weight, (start,), (rows,))
    ids_r, scale_r = spread(recv_order, [ids, scale])
    packed = jnp.stack([ids_r.reshape(n_chan, quota), scale_r.reshape(n_chan, quota)], axis=1)
    packed = lax.all_to_all(packed, "chan", split_axis=0, concat_axis=0, tiled=True)
    ids_u, scale_u = packed[:, 0].reshape(rows), packed[:, 1].reshape(rows)
    ids_p, scale_p = spread(send_order, [ids_u, scale_u])
    ids_p = jnp.broadcast_to(ids_p[:, None], (rows, 128))
    scale_p = jnp.broadcast_to(scale_p[:, None], (rows, 128))
    pieces = interaction.reshape(4, 4, G, 128, 512)
    anyspace = pl.BlockSpec(memory_space=pl.ANY)
    vmem = pl.BlockSpec(memory_space=pltpu.VMEM)
    return pl.pallas_call(
        kernel,
        out_shape=jax.ShapeDtypeStruct(t_pp.shape, BF),
        in_specs=[anyspace, anyspace, vmem, vmem],
        out_specs=anyspace,
        scratch_shapes=[
            pltpu.VMEM((4 * G * 16, 128, 512), BF),
            pltpu.VMEM((G, rows, 2048), BF),
            pltpu.VMEM((rows, 2048), BF),
            pltpu.VMEM((3, rows, 512), F32),
            pltpu.SemaphoreType.DMA((G + 1,)),
            pltpu.SemaphoreType.DMA((4,)),
            pltpu.SemaphoreType.DMA((7,)),
            pltpu.SemaphoreType.DMA((3 * G * 16,)),
        ],
        compiler_params=pltpu.CompilerParams(
            collective_id=0, has_side_effects=True, vmem_limit_bytes=66 * 1000 * 1000
        ),
    )(t_pp, pieces, ids_p, scale_p)


def solution(mesh):
    in_specs = (
        P(("chan", "int"), None),
        P(None, None, "int"),
        P(("chan", "int")),
        P(("chan", "int")),
        P("chan"),
        P("chan"),
    )
    out_specs = P(("chan", "int"), None)
    return jax.shard_map(
        on_device, mesh=mesh, in_specs=in_specs, out_specs=out_specs, check_vma=False
    )
```

time: 460 us -> 114 us (0.25)
  waiting for transfers between devices: 200 us -> 0 us
  blocking collectives: 107 us -> 15.7 us
  local copies, waits for them, and re-layouts: 59 us -> 7.87 us
  Pallas kernels: 50.3 us -> 85.3 us
  other arithmetic: 20.2 us -> 4.58 us
  between operations: 13.5 us -> 0.03 us
  starting transfers between devices: 8.8 us -> 0 us
    all_gather x1 -> x0, waiting for transfers between devices: 148 us -> none  [on_device(): everyone = lax.all_gather(ph_rows, 'int', axis=0, tiled=True)]
    all_to_all x2 -> x1, blocking collectives: 107 us -> 15.7 us  [on_device(): lax.all_to_all(packed, 'chan', split_axis=0, concat_axis=0, tiled=True)]
    pallas_call x0 -> x1, Pallas kernels: none -> 85.3 us  [on_device(): pl.pallas_call(kernel, out_shape=jax.ShapeDtypeStruct(t_pp.shape, BF), in...]
    all_to_all x1 -> x0, waiting for transfers between devices: 52 us -> none  [on_device(): lax.all_to_all(outgoing, 'chan', split_axis=0, concat_axis=0, tiled=True)]
    another operation x4 -> x0, Pallas kernels: 44.9 us -> none
    gather x2 -> x0, local copies, waits for them, and re-layouts: 23.1 us -> none  [the longest x1 11.5 us: on_device(): ph_rows = jnp.take(arrived, recv_order, axis=0)]
    scatter x2 -> x0, local copies, waits for them, and re-layouts: 20.2 us -> none  [the longest x1 10.1 us: on_device(): return jnp.zeros_like(returned).at[send_order].set(returned)]
    slice x3 -> x1, local copies, waits for them, and re-layouts: 12.4 us -> 0.09 us  [on_device(): ids_u, scale_u = (packed[:, 0].reshape(rows), packed[:, 1].reshape(rows))]
  transfers between devices with their start and end apart: 2 -> 0, of which waited for: 2 -> 0; matrix products, arithmetic and copies ran while one was open for 0% -> 0% of each run, Pallas kernels for 1% -> 0%
where the time goes in v1:
time: 114 us; the launch traced here: 113 us
  Pallas kernels  85.3 us (75%)
  blocking collectives  15.7 us (14%)
  local copies, waits for them, and re-layouts  7.87 us (7%)
  other arithmetic  4.58 us (4%)
    pallas_call x1, Pallas kernels, on_device(): pl.pallas_call(kernel, out_shape=jax.ShapeDtypeStruct(t_pp.shape, BF), in...  85.3 us
    all_to_all x1, blocking collectives, on_device(): lax.all_to_all(packed, 'chan', split_axis=0, concat_axis=0, tiled=True)  15.7 us
    unnamed x1, local copies, waits for them, and re-layouts  4.79 us
    reduce_sum x2, other arithmetic, spread(): jnp.sum(jnp.where(hit, v[None, :], jnp.float32(0.0)), axis=1)  3.85 us

profile of v1, /device:TPU:1, one launch (start us, length us, event | category | flops | bytes accessed | tf_op | source)
XLA Modules:
  0.0 113.5 jit_solution(9336077770977835388)
XLA Ops:
  0.0 0.7 dynamic-slice_convert_fusion
  0.7 0.7 dynamic_slice.7
  1.4 1.9 %select_reduce_fusion.3 = (f32[1024]{0:T(1024)S(1)}, f32[1024]{0:T(1024)S(1)}) fusion(f32[1024]{0:T(1024)S(1)} %dynamic-slice_convert_fusion, s32[1024]{0:T(1024)} %param.9, f32[1024]{0:T(1024)S(1)} %dynamic_slice.7), kind=kLoop, calls=%fused_computation.3 | loop fusion | flops 5240832 | bytes 20480 | tf_op jit(solution)/shard_map/reduce_sum | solution.py:17
  3.3 0.1 stack_reshape.6
  3.4 0.1 stack_reshape.7
  3.5 15.7 %all_to_all.5 = f32[32,2,32]{2,1,0:T(2,128)S(1)} all-to-all(f32[32,2,32]{2,1,0:T(2,128)S(1)} %pad_maximum_fusion), channel_id=1, replica_groups=mesh['chan'=32,'int'=4] {'chan'}, dimensions={0} | all-to-all | bytes 16384 | tf_op jit(solution)/shard_map/all_to_all | solution.py:203
  19.2 0.1 slice_reduce_fusion
  19.3 0.1 broadcast_in_dim.58
  19.4 0.1 broadcast_in_dim.55
  19.4 1.9 %select_reduce_fusion = (f32[1024]{0:T(1024)S(1)}, f32[1024]{0:T(1024)S(1)}) fusion(f32[1024]{0:T(1024)S(1)} %broadcast_in_dim.58, s32[1024]{0:T(1024)} %param.8, f32[1024]{0:T(1024)S(1)} %broadcast_in_dim.55), kind=kLoop, calls=%fused_computation | loop fusion | flops 5240832 | bytes 20480 | tf_op jit(solution)/shard_map/reduce_sum | solution.py:17
  21.3 1.0 broadcast_in_dim.60.scale_ref
  22.3 1.0 broadcast_in_dim.57.ch_ref
  23.3 85.3 %shard_map.64 = bf16[1024,2048]{1,0:T(8,128)(2,1)} custom-call(bf16[1024,2048]{1,0:T(8,128)(2,1)} %t_hbm.1, bf16[4,4,4,128,512]{4,3,2,1,0:T(8,128)(2,1)} %bitcast.1, f32[1024,128]{1,0:T(8,128)} %broadcast_in_dim.57.ch_ref, f32[1024,128]{1,0:T(8,128)} %broadcast_in_dim.60.scale_ref), custom_call_target="tpu_custom_call" | custom-call | tf_op jit(solution)/shard_map/pallas_call | solution.py:211
  108.7 4.8 %copy.8 = bf16[1024,2048]{1,0:T(8,128)(2,1)} copy(bf16[1024,2048]{1,0:T(8,128)(2,1)} %shard_map.64) | data formatting | bytes 8388608
  (1 shorter events, 0.0 us)

commit v2 on v1

v2 whole, which is shorter than its diff:
```python
import jax
import jax.numpy as jnp
from jax import lax
from jax.experimental import pallas as pl
from jax.experimental.pallas import tpu as pltpu
from jax.sharding import PartitionSpec as P

NX, NY, NCORE, NZ = 4, 4, 2, 4
G = 4
LB, LC, LD = 1, 2, 3
MESH = pl.DeviceIdType.MESH
BF = jnp.bfloat16
F32 = jnp.float32


def kernel(
    t_hbm, w_hbm, meta_hbm, order_ref, out_hbm,
    wbuf, tm, tbuf, acc, chb, scb, mb, mc, md,
    local_sem, out_sem, send_sem, recv_sem, msend, mrecv,
):
    rows, width = t_hbm.shape
    chan = lax.axis_index("chan")
    z = lax.axis_index("int")
    core = chan % NCORE
    y = (chan // NCORE) % NY
    x = chan // (NCORE * NY)

    def at_xy(px, py, pc):
        return {"chan": (px * NY + py) * NCORE + pc}

    xs = [at_xy((x + d) % NX, y, core) for d in (1, 2, 3)]
    ys = [at_xy(x, (y + d) % NY, core) for d in (1, 2, 3)]
    zp, zm = {"int": (z + 1) % NZ}, {"int": (z + NZ - 1) % NZ}
    sib = at_xy(x, y, 1 - core)
    links = (xs[0], xs[2], ys[0], ys[2], zp, zm, sib)
    XP, XM, YP, YM, ZP, ZM, SIB = range(7)
    steps = 3 * G

    t_copy = pltpu.make_async_copy(t_hbm, tbuf, local_sem.at[G])
    t_copy.start()
    keep_core = pltpu.make_async_copy(meta_hbm.at[:, :, core], mb.at[:, :, core], msend.at[7])
    keep_core.start()

    barrier = pltpu.get_barrier_semaphore()
    peers = [sib, zp, zm] + xs + ys
    for peer in peers:
        pl.semaphore_signal(barrier, inc=1, device_id=peer, device_id_type=MESH)
    pl.semaphore_wait(barrier, len(peers))

    def spot(dq, g, c, kq):
        return ((dq * G + g) * 4 + c) * 4 + kq

    def send(link, src, dst, index):
        pltpu.make_async_remote_copy(
            src_ref=src,
            dst_ref=dst,
            send_sem=send_sem.at[link],
            recv_sem=recv_sem.at[index - G * 16],
            device_id=links[link],
            device_id_type=MESH,
        ).start()

    def forward(link, index):
        send(link, wbuf.at[index], wbuf.at[index], index)

    def arrive(index):
        pltpu.make_async_copy(wbuf.at[index], wbuf.at[index], recv_sem.at[index - G * 16]).wait()

    def tell(src, dst, slot, device):
        return pltpu.make_async_remote_copy(
            src_ref=src, dst_ref=dst, send_sem=msend.at[slot], recv_sem=mrecv.at[slot],
            device_id=device, device_id_type=MESH,
        )

    cx, cy = 2 * core, 2 * core + 1

    def send_own(g):
        for c, kq in ((cx, x), (cy, y)):
            up, down = spot(3, g, c, kq), spot(1, g, c, kq)
            send(ZP, w_hbm.at[c, kq, g], wbuf.at[up], up)
            send(ZM, w_hbm.at[c, kq, g], wbuf.at[down], down)

    send_own(0)
    tells = [tell(meta_hbm.at[:, :, 1 - core], mb.at[:, :, core], 0, sib)]
    tells[0].start()
    for g in range(1, G):
        send_own(g)
    for g in range(G):
        for c in range(4):
            pltpu.make_async_copy(w_hbm.at[c, :, g], wbuf.at[pl.ds(g * 16 + c * 4, 4)], local_sem.at[g]).start()
    keep_core.wait()
    tells[0].wait_recv()
    for d in (1, 2, 3):
        tells.append(tell(mb.at[:, (y + d) % NY], mc.at[:, y], d, ys[d - 1]))
        tells[-1].start()
    keep_y = pltpu.make_async_copy(mb.at[:, y], mc.at[:, y], msend.at[8])
    keep_y.start()
    keep_y.wait()
    for d in (1, 2, 3):
        tells[d].wait_recv()
    for d in (1, 2, 3):
        tells.append(tell(mc.at[(x + d) % NX], md.at[x], 3 + d, xs[d - 1]))
        tells[-1].start()
    keep_x = pltpu.make_async_copy(mc.at[x], md.at[x], msend.at[9])
    keep_x.start()
    keep_x.wait()
    for d in (4, 5, 6):
        tells[d].wait_recv()

    @pl.loop(0, rows // 128)
    def _(m):
        first = m * 128
        row = lax.broadcasted_iota(jnp.int32, (128, 128), 0) + first
        ids = jnp.zeros((128, 128), F32)
        scale = jnp.zeros((128, 128), F32)
        for i in range(8):
            pair = md[i // 2, (i % 2) * 2, 0] + md[i // 2, (i % 2) * 2, 1]
            pair = pair + (md[i // 2, (i % 2) * 2 + 1, 0] + md[i // 2, (i % 2) * 2 + 1, 1])
            hit = row == order_ref[i : i + 1, :]
            ids = ids + jnp.where(hit, pair[0:1, :], jnp.float32(0.0))
            scale = scale + jnp.where(hit, pair[1:2, :], jnp.float32(0.0))
        r = pl.ds(pl.multiple_of(first, 128), 128)
        chb[r, :] = jnp.broadcast_to(jnp.sum(ids, axis=1, keepdims=True), (128, 128))
        scb[r, :] = jnp.broadcast_to(jnp.sum(scale, axis=1, keepdims=True), (128, 128))

    t_copy.wait()

    def mask_rows(g):
        @pl.loop(0, rows // 128)
        def _(m):
            r = pl.ds(pl.multiple_of(m * 128, 128), 128)
            for c in range(4):
                keep = jnp.where(chb[r, :] == jnp.float32(c), jnp.float32(1.0), jnp.float32(0.0)).astype(BF)
                for kq in range(4):
                    v = tbuf[r, pl.ds(pl.multiple_of((kq * G + g) * 128, 128), 128)]
                    tm[g, r, (c * 4 + kq) * 128 : (c * 4 + kq + 1) * 128] = v * keep

    def place(s):
        early = 1 - s // (2 * G)
        dq = early * (1 + 2 * (s % 2)) + (1 - early) * 2
        g = early * (s // 2) + (1 - early) * (s - 2 * G)
        return dq, g

    def unit(dq, g, slot):
        @pl.when(g == 0)
        def _():
            acc[slot] = jnp.zeros((rows, 512), F32)

        rhs = wbuf[pl.ds((dq * G + g) * 16, 16)].reshape(2048, 512)
        acc[slot] += jnp.dot(tm[g], rhs, preferred_element_type=F32)

        @pl.when(g == G - 1)
        def _():
            first = ((z + dq) % NZ) * 512
            col = pl.ds(pl.multiple_of(first, 512), 512)

            @pl.loop(0, rows // 128)
            def _(m):
                r = pl.ds(pl.multiple_of(m * 128, 128), 128)
                for part in range(4):
                    lanes = pl.ds(pl.multiple_of(first + part * 128, 128), 128)
                    obuf[r, lanes] = (acc[slot, r, part * 128 : (part + 1) * 128] * scb[r, :]).astype(BF)

            pltpu.make_async_copy(obuf.at[:, col], out_hbm.at[:, col], out_sem.at[dq]).start()

    obuf = tbuf

    def step(s, carry):
        @pl.when(s < steps)
        def _():
            dq, g = place(s)
            for c, kq, plus, minus in ((cx, x, XP, XM), (cy, y, YP, YM)):
                index = spot(dq, g, c, kq)
                arrive(index)
                forward(plus, index)
                forward(minus, index)
                forward(SIB, index)

            @pl.when(dq == 3)
            def _():
                index = spot(2, g, cx, x)
                send(ZP, wbuf.at[spot(3, g, cx, x)], wbuf.at[index], index)

            @pl.when(dq == 1)
            def _():
                index = spot(2, g, cy, y)
                send(ZM, wbuf.at[spot(1, g, cy, y)], wbuf.at[index], index)

        @pl.when(jnp.logical_and(s >= LB, s < steps + LB))
        def _():
            dq, g = place(s - LB)
            for c, kq, plus, minus in ((cx, x, XP, XM), (cy, y, YP, YM)):
                below, above = spot(dq, g, c, (kq + 3) % 4), spot(dq, g, c, (kq + 1) % 4)
                arrive(below)
                arrive(above)
                send(plus, wbuf.at[below, 0:64], wbuf.at[below, 0:64], below)
                send(minus, wbuf.at[above, 64:128], wbuf.at[above, 64:128], above)
                forward(SIB, below)
                forward(SIB, above)

        @pl.when(s < G)
        def _():
            mask_rows(s)
            own = wbuf.at[pl.ds(s * 16, 16)]
            pltpu.make_async_copy(own, own, local_sem.at[s]).wait()
            unit(0, s, 1)

        @pl.when(s >= LD)
        def _():
            dq, g = place(s - LD)
            for c in (2 - 2 * core, 3 - 2 * core):
                for kq in range(4):
                    arrive(spot(dq, g, c, kq))
            unit(dq, g, dq - 1)

        @pl.when(jnp.logical_and(s >= LC, s < steps + LC))
        def _():
            dq, g = place(s - LC)
            for c, kq in ((cx, x), (cy, y)):
                index = spot(dq, g, c, (kq + 2) % 4)
                arrive(index)
                forward(SIB, index)

        return carry

    lax.fori_loop(0, steps + LD, step, 0)

    for link, count in ((XP, 18), (XM, 18), (YP, 18), (YM, 18), (ZP, 12), (ZM, 12), (SIB, 96)):
        whole = wbuf.at[pl.ds(0, count * G // 4)]
        pltpu.make_async_copy(whole, whole, send_sem.at[link]).wait()
    for one in tells:
        one.wait_send()
    for dq in range(4):
        part = pl.ds(0, 512)
        pltpu.make_async_copy(tbuf.at[:, part], out_hbm.at[:, part], out_sem.at[dq]).wait()


def slot_values(recv_order, ph_channel, recouple_weight, rows):
    start = lax.axis_index("int") * rows
    ids = lax.dynamic_slice(ph_channel, (start,), (rows,)).astype(F32)
    scale = lax.dynamic_slice(recouple_weight, (start,), (rows,))
    hit = recv_order[None, :] == jnp.arange(rows, dtype=jnp.int32)[:, None]
    both = [jnp.sum(jnp.where(hit, v[None, :], jnp.float32(0.0)), axis=1) for v in (ids, scale)]
    quota = rows // lax.axis_size("chan")
    lanes = jnp.stack(both).reshape(2, NX, NY, NCORE, quota).transpose(1, 2, 3, 0, 4)
    mine = (jnp.arange(128) // quota) == lax.axis_index("chan") % (128 // quota)
    return jnp.where(mine, jnp.tile(lanes, (1, 1, 1, 1, 128 // quota)), jnp.float32(0.0))


def on_device(t_pp, interaction, send_order, recv_order, ph_channel, recouple_weight):
    rows = t_pp.shape[0]
    meta = slot_values(recv_order, ph_channel, recouple_weight, rows)
    pieces = interaction.reshape(4, 4, G, 128, 512)
    anyspace = pl.BlockSpec(memory_space=pl.ANY)
    vmem = pl.BlockSpec(memory_space=pltpu.VMEM)
    meta_shape = (NX, NY, NCORE, 2, 128)
    return pl.pallas_call(
        kernel,
        out_shape=jax.ShapeDtypeStruct(t_pp.shape, BF),
        in_specs=[anyspace, anyspace, anyspace, vmem],
        out_specs=anyspace,
        scratch_shapes=[
            pltpu.VMEM((4 * G * 16, 128, 512), BF),
            pltpu.VMEM((G, rows, 2048), BF),
            pltpu.VMEM((rows, 2048), BF),
            pltpu.VMEM((3, rows, 512), F32),
            pltpu.VMEM((rows, 128), F32),
            pltpu.VMEM((rows, 128), F32),
            pltpu.VMEM(meta_shape, F32),
            pltpu.VMEM(meta_shape, F32),
            pltpu.VMEM(meta_shape, F32),
            pltpu.SemaphoreType.DMA((G + 1,)),
            pltpu.SemaphoreType.DMA((4,)),
            pltpu.SemaphoreType.DMA((7,)),
            pltpu.SemaphoreType.DMA((3 * G * 16,)),
            pltpu.SemaphoreType.DMA((10,)),
            pltpu.SemaphoreType.DMA((7,)),
        ],
        compiler_params=pltpu.CompilerParams(
            collective_id=0, has_side_effects=True, vmem_limit_bytes=66 * 1000 * 1000
        ),
    )(t_pp, pieces, meta, send_order.reshape(rows // 128, 128))


def solution(mesh):
    in_specs = (
        P(("chan", "int"), None),
        P(None, None, "int"),
        P(("chan", "int")),
        P(("chan", "int")),
        P("chan"),
        P("chan"),
    )
    out_specs = P(("chan", "int"), None)
    return jax.shard_map(
        on_device, mesh=mesh, in_specs=in_specs, out_specs=out_specs, check_vma=False
    )
```

time: 114 us -> 93.3 us (0.82)
  blocking collectives: 15.7 us -> 0 us
  local copies, waits for them, and re-layouts: 7.87 us -> 5.81 us
  Pallas kernels: 85.3 us -> 83.9 us
  other arithmetic: 4.58 us -> 3.3 us
    all_to_all x1 -> x0, blocking collectives: 15.7 us -> none  [on_device(): lax.all_to_all(packed, 'chan', split_axis=0, concat_axis=0, tiled=True)]
    broadcast_in_dim x4 -> x0, local copies, waits for them, and re-layouts: 2.13 us -> none  [the longest x1 1 us: on_device(): scale_p = jnp.broadcast_to(scale_p[:, None], (rows, 128))]
    reduce_sum x2 -> x1, other arithmetic: 3.85 us -> 1.93 us  [slot_values(): jnp.sum(jnp.where(hit, v[None, :], jnp.float32(0.0)), axis=1)]
    pallas_call x1, Pallas kernels: 85.3 us -> 83.9 us  [on_device(): pl.pallas_call(kernel, out_shape=jax.ShapeDtypeStruct(t_pp.shape, BF), in...]
where the time goes in v2:
time: 93.3 us; the launch traced here: 93 us
  Pallas kernels  83.9 us (90%)
  local copies, waits for them, and re-layouts  5.81 us (6%)
  other arithmetic  3.3 us (4%)
    pallas_call x1, Pallas kernels, on_device(): pl.pallas_call(kernel, out_shape=jax.ShapeDtypeStruct(t_pp.shape, BF), in...  83.9 us
    unnamed x1, local copies, waits for them, and re-layouts  4.79 us
    reduce_sum x1, other arithmetic, slot_values(): jnp.sum(jnp.where(hit, v[None, :], jnp.float32(0.0)), axis=1)  1.93 us

profile of v2, /device:TPU:1, one launch (start us, length us, event | category | flops | bytes accessed | tf_op | source)
XLA Modules:
  0.0 93.0 jit_solution(482050574222601730)
XLA Ops:
  0.0 0.7 dynamic-slice_convert_fusion
  0.7 0.7 dynamic_slice.7
  1.4 1.9 %select_reduce_fusion.1 = (f32[1024]{0:T(1024)S(1)}, f32[1024]{0:T(1024)S(1)}) fusion(f32[1024]{0:T(1024)S(1)} %dynamic-slice_convert_fusion, s32[1024]{0:T(1024)} %param.9, f32[1024]{0:T(1024)S(1)} %dynamic_slice.7), kind=kLoop, calls=%fused_computation.1 | loop fusion | flops 5240832 | bytes 20480 | tf_op jit(solution)/shard_map/reduce_sum | solution.py:243
  3.3 0.1 stack.9
  3.4 0.1 stack.10
  3.6 0.1 tile.10
  3.7 0.6 broadcast_select_fusion.meta_hbm
  4.3 83.9 %shard_map.64 = bf16[1024,2048]{1,0:T(8,128)(2,1)} custom-call(bf16[1024,2048]{1,0:T(8,128)(2,1)} %t_hbm.1, bf16[4,4,4,128,512]{4,3,2,1,0:T(8,128)(2,1)} %bitcast.4, f32[4,4,2,2,128]{4,3,2,1,0:T(2,128)} %broadcast_select_fusion.meta_hbm, s32[8,128]{1,0:T(8,128)} %bitcast.5), custom_call_target="tpu_custom_call" | custom-call | tf_op jit(solution)/shard_map/pallas_call | solution.py:257
  88.2 4.8 %copy.8 = bf16[1024,2048]{1,0:T(8,128)(2,1)} copy(bf16[1024,2048]{1,0:T(8,128)(2,1)} %shard_map.64) | data formatting | bytes 8388608
  (3 shorter events, 0.1 us)

commit v3 on v2

v3 whole, which is shorter than its diff:
```python
import jax
import jax.numpy as jnp
from jax import lax
from jax.experimental import pallas as pl
from jax.experimental.pallas import tpu as pltpu
from jax.sharding import PartitionSpec as P

NX, NY, NCORE, NZ = 4, 4, 2, 4
G, GK, NB = 8, 4, 256
LEAD, LC, LD, PURE, PURE_IN = 4, 3, 5, 8, 16
KINDS = 7
MESH = pl.DeviceIdType.MESH
BF = jnp.bfloat16
F32 = jnp.float32


def kernel(
    t_hbm, w_hbm, meta_hbm, order_ref, out_hbm,
    wbuf, tm, tbuf, acc, chb, scb, mb, mc, md,
    local_sem, out_sem, send_sem, recv_sem, msend, mrecv,
):
    rows, width = t_hbm.shape
    chan = lax.axis_index("chan")
    z = lax.axis_index("int")
    core = chan % NCORE
    y = (chan // NCORE) % NY
    x = chan // (NCORE * NY)

    def at_xy(px, py, pc):
        return {"chan": (px * NY + py) * NCORE + pc}

    xs = [at_xy((x + d) % NX, y, core) for d in (1, 2, 3)]
    ys = [at_xy(x, (y + d) % NY, core) for d in (1, 2, 3)]
    zp, zm = {"int": (z + 1) % NZ}, {"int": (z + NZ - 1) % NZ}
    sib = at_xy(x, y, 1 - core)
    links = (xs[0], xs[2], ys[0], ys[2], zp, zm, sib)
    XP, XM, YP, YM, ZP, ZM, SIB = range(7)
    ring = G - 1
    steps = 3 * ring
    obuf = tbuf

    t_copy = pltpu.make_async_copy(t_hbm, tbuf, local_sem.at[G])
    t_copy.start()
    keep_core = pltpu.make_async_copy(meta_hbm.at[:, :, core], mb.at[:, :, core], msend.at[7])
    keep_core.start()

    barrier = pltpu.get_barrier_semaphore()
    peers = [sib, zp, zm] + xs + ys
    for peer in peers:
        pl.semaphore_signal(barrier, inc=1, device_id=peer, device_id_type=MESH)
    pl.semaphore_wait(barrier, len(peers))

    def spot(dq, g, c, kq):
        return ((dq * G + g) * 4 + c) * 4 + kq

    def send(link, src, index, kind, rows_of=None):
        dst = wbuf.at[index] if rows_of is None else wbuf.at[index, rows_of[0] : rows_of[1]]
        pltpu.make_async_remote_copy(
            src_ref=src,
            dst_ref=dst,
            send_sem=send_sem.at[link],
            recv_sem=recv_sem.at[(index // 16 - G) * KINDS + kind],
            device_id=links[link],
            device_id_type=MESH,
        ).start()

    def forward(link, index, kind):
        send(link, wbuf.at[index], index, kind)

    def arrive(index, kind, count=1):
        whole = wbuf.at[pl.ds(index, count)]
        pltpu.make_async_copy(whole, whole, recv_sem.at[(index // 16 - G) * KINDS + kind]).wait()

    def tell(src, dst, slot, device):
        return pltpu.make_async_remote_copy(
            src_ref=src, dst_ref=dst, send_sem=msend.at[slot], recv_sem=mrecv.at[slot],
            device_id=device, device_id_type=MESH,
        )

    cx, cy = 2 * core, 2 * core + 1

    def piece(c, kq, g):
        return w_hbm.at[c, kq, g % GK, :, pl.ds((g // GK) * NB, NB)]

    def send_own(link, dq, c, kq, g, kind):
        send(link, piece(c, kq, g), spot(dq, g, c, kq), kind)

    def send_ring(g):
        send_own(ZP, 3, cx, x, g, 1)
        send_own(ZM, 1, cy, y, g, 2)
        send_own(ZP, 3, cy, y, g, 2)
        send_own(ZM, 1, cx, x, g, 1)

    send_ring(0)
    tells = [tell(meta_hbm.at[:, :, 1 - core], mb.at[:, :, core], 0, sib)]
    tells[0].start()
    for g in range(1, ring):
        send_ring(g)
    for g in range(G):
        for c in range(4):
            src = w_hbm.at[c, :, g % GK, :, pl.ds((g // GK) * NB, NB)]
            pltpu.make_async_copy(src, wbuf.at[pl.ds(g * 16 + c * 4, 4)], local_sem.at[g]).start()
    keep_core.wait()
    tells[0].wait_recv()
    for d in (1, 2, 3):
        tells.append(tell(mb.at[:, (y + d) % NY], mc.at[:, y], d, ys[d - 1]))
        tells[-1].start()
    keep_y = pltpu.make_async_copy(mb.at[:, y], mc.at[:, y], msend.at[8])
    keep_y.start()
    keep_y.wait()
    for d in (1, 2, 3):
        tells[d].wait_recv()
    for d in (1, 2, 3):
        tells.append(tell(mc.at[(x + d) % NX], md.at[x], 3 + d, xs[d - 1]))
        tells[-1].start()
    keep_x = pltpu.make_async_copy(mc.at[x], md.at[x], msend.at[9])
    keep_x.start()

    def place(s, along_y):
        early = 1 - s // (2 * ring)
        odd = (s + along_y) % 2
        dq = early * (3 - 2 * odd) + (1 - early) * 2
        g = early * (s // 2) + (1 - early) * (s - 2 * ring)
        return dq, g

    def first_arrivals(s):
        for along_y, c, kq, plus, minus in ((0, cx, x, XP, XM), (1, cy, y, YP, YM)):
            dq, g = place(s, along_y)
            index = spot(dq, g, c, kq)
            arrive(index, 1 + along_y)
            forward(plus, index, 3 + along_y)
            forward(minus, index, 3 + along_y)
            forward(SIB, index, 0)

        @pl.when(jnp.logical_and(s % 2 == 0, s < 2 * ring))
        def _():
            g = s // 2
            send(ZP, wbuf.at[spot(3, g, cx, x)], spot(2, g, cx, x), 1)
            send(ZM, wbuf.at[spot(1, g, cy, y)], spot(2, g, cy, y), 2)

    for s in range(2):
        first_arrivals(jnp.int32(s))

    keep_x.wait()
    for d in (4, 5, 6):
        tells[d].wait_recv()

    @pl.loop(0, rows // 128)
    def _(m):
        first = m * 128
        row = lax.broadcasted_iota(jnp.int32, (128, 128), 0) + first
        ids = jnp.zeros((128, 128), F32)
        scale = jnp.zeros((128, 128), F32)
        for i in range(8):
            pair = md[i // 2, (i % 2) * 2, 0] + md[i // 2, (i % 2) * 2, 1]
            pair = pair + (md[i // 2, (i % 2) * 2 + 1, 0] + md[i // 2, (i % 2) * 2 + 1, 1])
            hit = row == order_ref[i : i + 1, :]
            ids = ids + jnp.where(hit, pair[0:1, :], jnp.float32(0.0))
            scale = scale + jnp.where(hit, pair[1:2, :], jnp.float32(0.0))
        r = pl.ds(pl.multiple_of(first, 128), 128)
        chb[r, :] = jnp.broadcast_to(jnp.sum(ids, axis=1, keepdims=True), (128, 128))
        scb[r, :] = jnp.broadcast_to(jnp.sum(scale, axis=1, keepdims=True), (128, 128))

    t_copy.wait()

    def mask_rows(g):
        @pl.loop(0, rows // 128)
        def _(m):
            r = pl.ds(pl.multiple_of(m * 128, 128), 128)
            for c in range(4):
                keep = jnp.where(chb[r, :] == jnp.float32(c), jnp.float32(1.0), jnp.float32(0.0)).astype(BF)
                for kq in range(4):
                    v = tbuf[r, pl.ds(pl.multiple_of((kq * GK + g) * 128, 128), 128)]
                    tm[g, r, (c * 4 + kq) * 128 : (c * 4 + kq + 1) * 128] = v * keep

    def unit(dq, g, slot):
        gk = g % GK
        nh = g // GK
        cols = pl.ds(pl.multiple_of(nh * NB, NB), NB)

        @pl.when(gk == 0)
        def _():
            acc[slot, :, cols] = jnp.zeros((rows, NB), F32)

        rhs = wbuf[pl.ds((dq * G + g) * 16, 16)].reshape(2048, NB)
        acc[slot, :, cols] += jnp.dot(tm[gk], rhs, preferred_element_type=F32)

        @pl.when(gk == GK - 1)
        def _():
            first = ((z + dq) % NZ) * 512 + nh * NB
            col = pl.ds(pl.multiple_of(first, NB), NB)

            @pl.loop(0, rows // 128)
            def _(m):
                r = pl.ds(pl.multiple_of(m * 128, 128), 128)
                for part in range(NB // 128):
                    src = pl.ds(pl.multiple_of(nh * NB + part * 128, 128), 128)
                    dst = pl.ds(pl.multiple_of(first + part * 128, 128), 128)
                    obuf[r, dst] = (acc[slot, r, src] * scb[r, :]).astype(BF)

            pltpu.make_async_copy(obuf.at[:, col], out_hbm.at[:, col], out_sem.at[dq * 2 + nh]).start()

    def work(dq, g):
        arrive(spot(dq, g, 2 - 2 * core, 0), 0, 8)
        unit(dq, g, dq - 1)

    def step(s, carry):
        grown = jnp.minimum(s // 2, LEAD - 2)
        count = 1 + (s % 2) * (1 - jnp.minimum(s // (2 * (LEAD - 2)), 1))
        count = jnp.maximum(jnp.minimum(count, steps - (s + 2 + grown)), 0)

        def more(k, inner):
            first_arrivals(s + 2 + grown + k)
            return inner

        lax.fori_loop(0, count, more, 0)

        @pl.when(s < steps)
        def _():
            for along_y, c, kq, plus, minus in ((0, cx, x, XP, XM), (1, cy, y, YP, YM)):
                dq, g = place(s, along_y)
                below, above = spot(dq, g, c, (kq + 3) % 4), spot(dq, g, c, (kq + 1) % 4)
                arrive(spot(dq, g, c, 0), 3 + along_y, 2)
                send(plus, wbuf.at[below, 0:64], below, 5 + along_y, (0, 64))
                send(minus, wbuf.at[above, 64:128], above, 5 + along_y, (64, 128))
                forward(SIB, below, 0)
                forward(SIB, above, 0)

        @pl.when(s == PURE)
        def _():
            for kq in range(4):
                for c in (cx, cy):
                    send_own(ZP, 3, c, kq, G - 1, 1 + kq)
                    send_own(ZM, 1, c, kq, G - 1, 1 + kq)

        @pl.when(jnp.logical_and(s >= PURE_IN, s < PURE_IN + 4))
        def _():
            kq = s - PURE_IN
            for dq in (3, 1):
                arrive(spot(dq, G - 1, 0, 0), 1 + kq, 2)
            send(ZP, wbuf.at[spot(3, G - 1, cx, kq)], spot(2, G - 1, cx, kq), 1 + kq)
            send(ZM, wbuf.at[spot(1, G - 1, cy, kq)], spot(2, G - 1, cy, kq), 1 + kq)
            for dq in (3, 1):
                for c in (cx, cy):
                    forward(SIB, spot(dq, G - 1, c, kq), 0)

        @pl.when(s < G)
        def _():
            @pl.when(s < GK)
            def _():
                mask_rows(s)

            own = wbuf.at[pl.ds(s * 16, 16)]
            pltpu.make_async_copy(own, own, local_sem.at[s]).wait()
            unit(0, s, 1)

        @pl.when(s >= LD)
        def _():
            work(*place(s - LD, 0))

        @pl.when(jnp.logical_and(s >= steps, s < steps + 2))
        def _():
            work(3 - 2 * (s - steps), G - 1)

        @pl.when(jnp.logical_and(s >= LC, s < steps + LC))
        def _():
            for along_y, c, kq in ((0, cx, x), (1, cy, y)):
                dq, g = place(s - LC, along_y)
                index = spot(dq, g, c, (kq + 2) % 4)
                arrive(index, 5 + along_y)
                forward(SIB, index, 0)

        return carry

    lax.fori_loop(0, steps + LC, step, 0)

    for kq in range(4):
        arrive(spot(2, G - 1, 0, 0), 1 + kq, 2)
        for c in (cx, cy):
            forward(SIB, spot(2, G - 1, c, kq), 0)

    def rest(g, carry):
        work(2, g)
        return carry

    lax.fori_loop(ring - (LD - LC), G, rest, 0)

    for link in (XP, XM, YP, YM):
        whole = wbuf.at[pl.ds(0, steps * 3), 0:64]
        pltpu.make_async_copy(whole, whole, send_sem.at[link]).wait()
    for link, count in ((ZP, steps + 12), (ZM, steps + 12), (SIB, 3 * G * 8)):
        whole = wbuf.at[pl.ds(0, count)]
        pltpu.make_async_copy(whole, whole, send_sem.at[link]).wait()
    for one in tells:
        one.wait_send()
    for part in range(8):
        cols = pl.ds(0, NB)
        pltpu.make_async_copy(obuf.at[:, cols], out_hbm.at[:, cols], out_sem.at[part]).wait()


def slot_values(recv_order, ph_channel, recouple_weight, rows):
    start = lax.axis_index("int") * rows
    ids = lax.dynamic_slice(ph_channel, (start,), (rows,)).astype(F32)
    scale = lax.dynamic_slice(recouple_weight, (start,), (rows,))
    hit = recv_order[None, :] == jnp.arange(rows, dtype=jnp.int32)[:, None]
    both = [jnp.sum(jnp.where(hit, v[None, :], jnp.float32(0.0)), axis=1) for v in (ids, scale)]
    quota = rows // lax.axis_size("chan")
    lanes = jnp.stack(both).reshape(2, NX, NY, NCORE, quota).transpose(1, 2, 3, 0, 4)
    mine = (jnp.arange(128) // quota) == lax.axis_index("chan") % (128 // quota)
    return jnp.where(mine, jnp.tile(lanes, (1, 1, 1, 1, 128 // quota)), jnp.float32(0.0))


def on_device(t_pp, interaction, send_order, recv_order, ph_channel, recouple_weight):
    rows = t_pp.shape[0]
    meta = slot_values(recv_order, ph_channel, recouple_weight, rows)
    pieces = interaction.reshape(4, 4, GK, 128, 512)
    anyspace = pl.BlockSpec(memory_space=pl.ANY)
    vmem = pl.BlockSpec(memory_space=pltpu.VMEM)
    meta_shape = (NX, NY, NCORE, 2, 128)
    return pl.pallas_call(
        kernel,
        out_shape=jax.ShapeDtypeStruct(t_pp.shape, BF),
        in_specs=[anyspace, anyspace, anyspace, vmem],
        out_specs=anyspace,
        scratch_shapes=[
            pltpu.VMEM((4 * G * 16, 128, NB), BF),
            pltpu.VMEM((GK, rows, 2048), BF),
            pltpu.VMEM((rows, 2048), BF),
            pltpu.VMEM((3, rows, 512), F32),
            pltpu.VMEM((rows, 128), F32),
            pltpu.VMEM((rows, 128), F32),
            pltpu.VMEM(meta_shape, F32),
            pltpu.VMEM(meta_shape, F32),
            pltpu.VMEM(meta_shape, F32),
            pltpu.SemaphoreType.DMA((G + 1,)),
            pltpu.SemaphoreType.DMA((8,)),
            pltpu.SemaphoreType.DMA((7,)),
            pltpu.SemaphoreType.DMA((3 * G * KINDS,)),
            pltpu.SemaphoreType.DMA((10,)),
            pltpu.SemaphoreType.DMA((7,)),
        ],
        compiler_params=pltpu.CompilerParams(
            collective_id=0, has_side_effects=True, vmem_limit_bytes=66 * 1000 * 1000
        ),
    )(t_pp, pieces, meta, send_order.reshape(rows // 128, 128))


def solution(mesh):
    in_specs = (
        P(("chan", "int"), None),
        P(None, None, "int"),
        P(("chan", "int")),
        P(("chan", "int")),
        P("chan"),
        P("chan"),
    )
    out_specs = P(("chan", "int"), None)
    return jax.shard_map(
        on_device, mesh=mesh, in_specs=in_specs, out_specs=out_specs, check_vma=False
    )
```

time: 93.3 us -> 88.7 us (0.951)
  Pallas kernels: 83.9 us -> 79.3 us
    pallas_call x1, Pallas kernels: 83.9 us -> 79.3 us  [on_device(): pl.pallas_call(kernel, out_shape=jax.ShapeDtypeStruct(t_pp.shape, BF), in...]
where the time goes in v3:
time: 88.7 us; the launch traced here: 88.5 us
  Pallas kernels  79.3 us (89%)
  local copies, waits for them, and re-layouts  5.81 us (7%)
  other arithmetic  3.3 us (4%)
    pallas_call x1, Pallas kernels, on_device(): pl.pallas_call(kernel, out_shape=jax.ShapeDtypeStruct(t_pp.shape, BF), in...  79.3 us
    unnamed x1, local copies, waits for them, and re-layouts  4.79 us
    reduce_sum x1, other arithmetic, slot_values(): jnp.sum(jnp.where(hit, v[None, :], jnp.float32(0.0)), axis=1)  1.93 us

profile of v3, /device:TPU:1, one launch (start us, length us, event | category | flops | bytes accessed | tf_op | source)
XLA Modules:
  0.0 88.5 jit_solution(14537289354600664545)
XLA Ops:
  0.0 0.7 dynamic-slice_convert_fusion
  0.7 0.7 dynamic_slice.7
  1.4 1.9 %select_reduce_fusion.1 = (f32[1024]{0:T(1024)S(1)}, f32[1024]{0:T(1024)S(1)}) fusion(f32[1024]{0:T(1024)S(1)} %dynamic-slice_convert_fusion, s32[1024]{0:T(1024)} %param.9, f32[1024]{0:T(1024)S(1)} %dynamic_slice.7), kind=kLoop, calls=%fused_computation.1 | loop fusion | flops 5240832 | bytes 20480 | tf_op jit(solution)/shard_map/reduce_sum | solution.py:306
  3.3 0.1 stack.9
  3.4 0.1 stack.10
  3.6 0.1 tile.10
  3.7 0.6 broadcast_select_fusion.meta_hbm
  4.3 79.3 %shard_map.64 = bf16[1024,2048]{1,0:T(8,128)(2,1)} custom-call(bf16[1024,2048]{1,0:T(8,128)(2,1)} %t_hbm.1, bf16[4,4,4,128,512]{4,3,2,1,0:T(8,128)(2,1)} %bitcast.4, f32[4,4,2,2,128]{4,3,2,1,0:T(2,128)} %broadcast_select_fusion.meta_hbm, s32[8,128]{1,0:T(8,128)} %bitcast.5), custom_call_target="tpu_custom_call" | custom-call | tf_op jit(solution)/shard_map/pallas_call | solution.py:320
  83.7 4.8 %copy.8 = bf16[1024,2048]{1,0:T(8,128)(2,1)} copy(bf16[1024,2048]{1,0:T(8,128)(2,1)} %shard_map.64) | data formatting | bytes 8388608
  (3 shorter events, 0.1 us)

commit v4 on v3

--- a/solution.py
+++ b/solution.py
@@ -7,7 +7,7 @@
 
 NX, NY, NCORE, NZ = 4, 4, 2, 4
 G, GK, NB = 8, 4, 256
-LEAD, LC, LD, PURE, PURE_IN = 4, 3, 5, 8, 16
+LEAD, LC, LD, PURE, PURE_IN = 5, 3, 5, 8, 16
 KINDS = 7
 MESH = pl.DeviceIdType.MESH
 BF = jnp.bfloat16
@@ -15,9 +15,9 @@
 
 
 def kernel(
-    t_hbm, w_hbm, meta_hbm, order_ref, out_hbm,
-    wbuf, tm, tbuf, acc, chb, scb, mb, mc, md,
-    local_sem, out_sem, send_sem, recv_sem, msend, mrecv,
+    t_hbm, w_hbm, meta_hbm, order_ref, out_ref,
+    own, wbuf, tm, acc, chb, scb, kb, mb, mc, md,
+    local_sem, send_sem, recv_sem, msend, mrecv,
 ):
     rows, width = t_hbm.shape
     chan = lax.axis_index("chan")
@@ -37,10 +37,11 @@
     XP, XM, YP, YM, ZP, ZM, SIB = range(7)
     ring = G - 1
     steps = 3 * ring
-    obuf = tbuf
-
-    t_copy = pltpu.make_async_copy(t_hbm, tbuf, local_sem.at[G])
+
+    t_copy = pltpu.make_async_copy(t_hbm, out_ref, local_sem.at[4])
     t_copy.start()
+    own_copies = [pltpu.make_async_copy(w_hbm.at[c], own.at[c], local_sem.at[c]) for c in range(4)]
+    own_copies[0].start()
     keep_core = pltpu.make_async_copy(meta_hbm.at[:, :, core], mb.at[:, :, core], msend.at[7])
     keep_core.start()
 
@@ -51,7 +52,7 @@
     pl.semaphore_wait(barrier, len(peers))
 
     def spot(dq, g, c, kq):
-        return ((dq * G + g) * 4 + c) * 4 + kq
+        return (((dq - 1) * G + g) * 4 + c) * 4 + kq
 
     def send(link, src, index, kind, rows_of=None):
         dst = wbuf.at[index] if rows_of is None else wbuf.at[index, rows_of[0] : rows_of[1]]
@@ -59,7 +60,7 @@
             src_ref=src,
             dst_ref=dst,
             send_sem=send_sem.at[link],
-            recv_sem=recv_sem.at[(index // 16 - G) * KINDS + kind],
+            recv_sem=recv_sem.at[(index // 16) * KINDS + kind],
             device_id=links[link],
             device_id_type=MESH,
         ).start()
@@ -69,7 +70,7 @@
 
     def arrive(index, kind, count=1):
         whole = wbuf.at[pl.ds(index, count)]
-        pltpu.make_async_copy(whole, whole, recv_sem.at[(index // 16 - G) * KINDS + kind]).wait()
+        pltpu.make_async_copy(whole, whole, recv_sem.at[(index // 16) * KINDS + kind]).wait()
 
     def tell(src, dst, slot, device):
         return pltpu.make_async_remote_copy(
@@ -96,10 +97,8 @@
     tells[0].start()
     for g in range(1, ring):
         send_ring(g)
-    for g in range(G):
-        for c in range(4):
-            src = w_hbm.at[c, :, g % GK, :, pl.ds((g // GK) * NB, NB)]
-            pltpu.make_async_copy(src, wbuf.at[pl.ds(g * 16 + c * 4, 4)], local_sem.at[g]).start()
+    for c in (1, 2, 3):
+        own_copies[c].start()
     keep_core.wait()
     tells[0].wait_recv()
     for d in (1, 2, 3):
@@ -107,6 +106,35 @@
         tells[-1].start()
     keep_y = pltpu.make_async_copy(mb.at[:, y], mc.at[:, y], msend.at[8])
     keep_y.start()
+
+    def place(s, along_y):
+        early = 1 - s // (2 * ring)
+        odd = (s + along_y) % 2
+        dq = early * (3 - 2 * odd) + (1 - early) * 2
+        g = early * (s // 2) + (1 - early) * (s - 2 * ring)
+        return dq, g
+
+    def first_arrivals(s):
+        for along_y, c, kq, plus, minus in ((0, cx, x, XP, XM), (1, cy, y, YP, YM)):
+            dq, g = place(s, along_y)
+            index = spot(dq, g, c, kq)
+            arrive(index, 1 + along_y)
+            forward(plus, index, 3 + along_y)
+            forward(minus, index, 3 + along_y)
+            forward(SIB, index, 0)
+
+        @pl.when(jnp.logical_and(s % 2 == 0, s < 2 * ring))
+        def _():
+            g = s // 2
+            send(ZP, wbuf.at[spot(3, g, cx, x)], spot(2, g, cx, x), 1)
+            send(ZM, wbuf.at[spot(1, g, cy, y)], spot(2, g, cy, y), 2)
+
+    def raw(c):
+        return jnp.dot(out_ref[...], own[c].reshape(2048, 512), preferred_element_type=F32)
+
+    t_copy.wait()
+    own_copies[0].wait()
+    acc[0] = raw(0)
     keep_y.wait()
     for d in (1, 2, 3):
         tells[d].wait_recv()
@@ -115,32 +143,12 @@
         tells[-1].start()
     keep_x = pltpu.make_async_copy(mc.at[x], md.at[x], msend.at[9])
     keep_x.start()
-
-    def place(s, along_y):
-        early = 1 - s // (2 * ring)
-        odd = (s + along_y) % 2
-        dq = early * (3 - 2 * odd) + (1 - early) * 2
-        g = early * (s // 2) + (1 - early) * (s - 2 * ring)
-        return dq, g
-
-    def first_arrivals(s):
-        for along_y, c, kq, plus, minus in ((0, cx, x, XP, XM), (1, cy, y, YP, YM)):
-            dq, g = place(s, along_y)
-            index = spot(dq, g, c, kq)
-            arrive(index, 1 + along_y)
-            forward(plus, index, 3 + along_y)
-            forward(minus, index, 3 + along_y)
-            forward(SIB, index, 0)
-
-        @pl.when(jnp.logical_and(s % 2 == 0, s < 2 * ring))
-        def _():
-            g = s // 2
-            send(ZP, wbuf.at[spot(3, g, cx, x)], spot(2, g, cx, x), 1)
-            send(ZM, wbuf.at[spot(1, g, cy, y)], spot(2, g, cy, y), 2)
-
-    for s in range(2):
+    for s in (0, 1):
         first_arrivals(jnp.int32(s))
-
+    own_copies[1].wait()
+    acc[1] = raw(1)
+    for s in (2, 3):
+        first_arrivals(jnp.int32(s))
     keep_x.wait()
     for d in (4, 5, 6):
         tells[d].wait_recv()
@@ -158,20 +166,37 @@
             ids = ids + jnp.where(hit, pair[0:1, :], jnp.float32(0.0))
             scale = scale + jnp.where(hit, pair[1:2, :], jnp.float32(0.0))
         r = pl.ds(pl.multiple_of(first, 128), 128)
-        chb[r, :] = jnp.broadcast_to(jnp.sum(ids, axis=1, keepdims=True), (128, 128))
+        ids = jnp.broadcast_to(jnp.sum(ids, axis=1, keepdims=True), (128, 128))
+        chb[r, :] = ids
+        for c in range(4):
+            kb[c, r, :] = jnp.where(ids == jnp.float32(c), jnp.float32(1.0), jnp.float32(0.0)).astype(BF)
         scb[r, :] = jnp.broadcast_to(jnp.sum(scale, axis=1, keepdims=True), (128, 128))
 
-    t_copy.wait()
+    own_copies[2].wait()
+    acc[2] = raw(2)
+    first_arrivals(jnp.int32(4))
 
     def mask_rows(g):
         @pl.loop(0, rows // 128)
         def _(m):
             r = pl.ds(pl.multiple_of(m * 128, 128), 128)
             for c in range(4):
-                keep = jnp.where(chb[r, :] == jnp.float32(c), jnp.float32(1.0), jnp.float32(0.0)).astype(BF)
                 for kq in range(4):
-                    v = tbuf[r, pl.ds(pl.multiple_of((kq * GK + g) * 128, 128), 128)]
-                    tm[g, r, (c * 4 + kq) * 128 : (c * 4 + kq + 1) * 128] = v * keep
+                    v = out_ref[r, pl.ds(pl.multiple_of((kq * GK + g) * 128, 128), 128)]
+                    tm[g, r, (c * 4 + kq) * 128 : (c * 4 + kq + 1) * 128] = v * kb[c, r, :]
+
+    def finish_own():
+        own_copies[3].wait()
+        wide = raw(3)
+        for m in range(rows // 128):
+            r = slice(m * 128, (m + 1) * 128)
+            ids, scale = chb[r, :], scb[r, :]
+            for part in range(4):
+                col = slice(part * 128, (part + 1) * 128)
+                v = jnp.where(ids == jnp.float32(3), wide[r, col], jnp.float32(0.0))
+                for c in range(3):
+                    v = jnp.where(ids == jnp.float32(c), acc[c, r, col], v)
+                out_ref[r, pl.ds(pl.multiple_of(z * 512 + part * 128, 128), 128)] = (v * scale).astype(BF)
 
     def unit(dq, g, slot):
         gk = g % GK
@@ -182,13 +207,12 @@
         def _():
             acc[slot, :, cols] = jnp.zeros((rows, NB), F32)
 
-        rhs = wbuf[pl.ds((dq * G + g) * 16, 16)].reshape(2048, NB)
+        rhs = wbuf[pl.ds(((dq - 1) * G + g) * 16, 16)].reshape(2048, NB)
         acc[slot, :, cols] += jnp.dot(tm[gk], rhs, preferred_element_type=F32)
 
         @pl.when(gk == GK - 1)
         def _():
             first = ((z + dq) % NZ) * 512 + nh * NB
-            col = pl.ds(pl.multiple_of(first, NB), NB)
 
             @pl.loop(0, rows // 128)
             def _(m):
@@ -196,24 +220,17 @@
                 for part in range(NB // 128):
                     src = pl.ds(pl.multiple_of(nh * NB + part * 128, 128), 128)
                     dst = pl.ds(pl.multiple_of(first + part * 128, 128), 128)
-                    obuf[r, dst] = (acc[slot, r, src] * scb[r, :]).astype(BF)
-
-            pltpu.make_async_copy(obuf.at[:, col], out_hbm.at[:, col], out_sem.at[dq * 2 + nh]).start()
+                    out_ref[r, dst] = (acc[slot, r, src] * scb[r, :]).astype(BF)
+
 
     def work(dq, g):
         arrive(spot(dq, g, 2 - 2 * core, 0), 0, 8)
         unit(dq, g, dq - 1)
 
     def step(s, carry):
-        grown = jnp.minimum(s // 2, LEAD - 2)
-        count = 1 + (s % 2) * (1 - jnp.minimum(s // (2 * (LEAD - 2)), 1))
-        count = jnp.maximum(jnp.minimum(count, steps - (s + 2 + grown)), 0)
-
-        def more(k, inner):
-            first_arrivals(s + 2 + grown + k)
-            return inner
-
-        lax.fori_loop(0, count, more, 0)
+        @pl.when(s + LEAD < steps)
+        def _():
+            first_arrivals(s + LEAD)
 
         @pl.when(s < steps)
         def _():
@@ -244,15 +261,13 @@
                 for c in (cx, cy):
                     forward(SIB, spot(dq, G - 1, c, kq), 0)
 
-        @pl.when(s < G)
-        def _():
-            @pl.when(s < GK)
-            def _():
-                mask_rows(s)
-
-            own = wbuf.at[pl.ds(s * 16, 16)]
-            pltpu.make_async_copy(own, own, local_sem.at[s]).wait()
-            unit(0, s, 1)
+        @pl.when(s < GK)
+        def _():
+            mask_rows(s)
+
+        @pl.when(s == GK)
+        def _():
+            finish_own()
 
         @pl.when(s >= LD)
         def _():
@@ -293,9 +308,6 @@
         pltpu.make_async_copy(whole, whole, send_sem.at[link]).wait()
     for one in tells:
         one.wait_send()
-    for part in range(8):
-        cols = pl.ds(0, NB)
-        pltpu.make_async_copy(obuf.at[:, cols], out_hbm.at[:, cols], out_sem.at[part]).wait()
 
 
 def slot_values(recv_order, ph_channel, recouple_weight, rows):
@@ -319,28 +331,28 @@
     meta_shape = (NX, NY, NCORE, 2, 128)
     return pl.pallas_call(
         kernel,
-        out_shape=jax.ShapeDtypeStruct(t_pp.shape, BF),
+        out_shape=pltpu.VMEM(t_pp.shape, BF),
         in_specs=[anyspace, anyspace, anyspace, vmem],
-        out_specs=anyspace,
+        out_specs=vmem,
         scratch_shapes=[
-            pltpu.VMEM((4 * G * 16, 128, NB), BF),
+            pltpu.VMEM((4, 4, GK, 128, 512), BF),
+            pltpu.VMEM((3 * G * 16, 128, NB), BF),
             pltpu.VMEM((GK, rows, 2048), BF),
-            pltpu.VMEM((rows, 2048), BF),
             pltpu.VMEM((3, rows, 512), F32),
             pltpu.VMEM((rows, 128), F32),
             pltpu.VMEM((rows, 128), F32),
+            pltpu.VMEM((4, rows, 128), BF),
             pltpu.VMEM(meta_shape, F32),
             pltpu.VMEM(meta_shape, F32),
             pltpu.VMEM(meta_shape, F32),
-            pltpu.SemaphoreType.DMA((G + 1,)),
-            pltpu.SemaphoreType.DMA((8,)),
+            pltpu.SemaphoreType.DMA((5,)),
             pltpu.SemaphoreType.DMA((7,)),
             pltpu.SemaphoreType.DMA((3 * G * KINDS,)),
             pltpu.SemaphoreType.DMA((10,)),
             pltpu.SemaphoreType.DMA((7,)),
         ],
         compiler_params=pltpu.CompilerParams(
-            collective_id=0, has_side_effects=True, vmem_limit_bytes=66 * 1000 * 1000
+            collective_id=0, has_side_effects=True, vmem_limit_bytes=62500000
         ),
     )(t_pp, pieces, meta, send_order.reshape(rows // 128, 128))
 

time: 88.7 us -> 83 us (0.936)
  Pallas kernels: 79.3 us -> 76.4 us
  local copies, waits for them, and re-layouts: 5.81 us -> 3.03 us
    pallas_call x1, Pallas kernels: 79.3 us -> 76.4 us  [on_device(): pl.pallas_call(kernel, out_shape=pltpu.VMEM(t_pp.shape, BF), in_specs=[an...]
    unnamed x1, local copies, waits for them, and re-layouts: 4.79 us -> 2.02 us
where the time goes in v4:
time: 83 us; the launch traced here: 82.8 us
  Pallas kernels  76.4 us (92%)
  other arithmetic  3.3 us (4%)
  local copies, waits for them, and re-layouts  3.03 us (4%)
    pallas_call x1, Pallas kernels, on_device(): pl.pallas_call(kernel, out_shape=pltpu.VMEM(t_pp.shape, BF), in_specs=[an...  76.4 us
    unnamed x1, local copies, waits for them, and re-layouts  2.02 us
    reduce_sum x1, other arithmetic, slot_values(): jnp.sum(jnp.where(hit, v[None, :], jnp.float32(0.0)), axis=1)  1.93 us

profile of v4, /device:TPU:1, one launch (start us, length us, event | category | flops | bytes accessed | tf_op | source)
XLA Modules:
  0.0 82.8 jit_solution(12915487904889476729)
XLA Ops:
  0.0 0.7 dynamic-slice_convert_fusion
  0.7 0.7 dynamic_slice.7
  1.4 1.9 %select_reduce_fusion.1 = (f32[1024]{0:T(1024)S(1)}, f32[1024]{0:T(1024)S(1)}) fusion(f32[1024]{0:T(1024)S(1)} %dynamic-slice_convert_fusion, s32[1024]{0:T(1024)} %param.9, f32[1024]{0:T(1024)S(1)} %dynamic_slice.7), kind=kLoop, calls=%fused_computation.1 | loop fusion | flops 5240832 | bytes 20480 | tf_op jit(solution)/shard_map/reduce_sum | solution.py:318
  3.3 0.1 stack.9
  3.4 0.1 stack.10
  3.6 0.1 tile.10
  3.7 0.6 broadcast_select_fusion.meta_hbm
  4.3 76.4 %shard_map.64 = bf16[1024,2048]{1,0:T(8,128)(2,1)S(1)} custom-call(bf16[1024,2048]{1,0:T(8,128)(2,1)} %t_hbm.1, bf16[4,4,4,128,512]{4,3,2,1,0:T(8,128)(2,1)} %bitcast.4, f32[4,4,2,2,128]{4,3,2,1,0:T(2,128)} %broadcast_select_fusion.meta_hbm, s32[8,128]{1,0:T(8,128)} %bitcast.5), custom_call_target="tpu_custom_call" | custom-call | tf_op jit(solution)/shard_map/pallas_call | solution.py:332
  80.8 2.0 %copy.8 = bf16[1024,2048]{1,0:T(8,128)(2,1)} copy(bf16[1024,2048]{1,0:T(8,128)(2,1)S(1)} %shard_map.64) | data formatting | bytes 8388608
  (3 shorter events, 0.1 us)

commit v5 on v4

--- a/solution.py
+++ b/solution.py
@@ -7,7 +7,7 @@
 
 NX, NY, NCORE, NZ = 4, 4, 2, 4
 G, GK, NB = 8, 4, 256
-LEAD, LC, LD, PURE, PURE_IN = 5, 3, 5, 8, 16
+LEAD, LC, LD, PURE, PURE_IN = 4, 2, 5, 5, 13
 KINDS = 7
 MESH = pl.DeviceIdType.MESH
 BF = jnp.bfloat16
@@ -174,7 +174,6 @@
 
     own_copies[2].wait()
     acc[2] = raw(2)
-    first_arrivals(jnp.int32(4))
 
     def mask_rows(g):
         @pl.loop(0, rows // 128)

time: 83 us -> 79.9 us (0.963)
  Pallas kernels: 76.4 us -> 73 us
    pallas_call x1, Pallas kernels: 76.4 us -> 73 us  [on_device(): pl.pallas_call(kernel, out_shape=pltpu.VMEM(t_pp.shape, BF), in_specs=[an...]
where the time goes in v5:
time: 79.9 us; the launch traced here: 79.3 us
  Pallas kernels  73 us (91%)
  other arithmetic  3.3 us (4%)
  local copies, waits for them, and re-layouts  3.03 us (4%)
    pallas_call x1, Pallas kernels, on_device(): pl.pallas_call(kernel, out_shape=pltpu.VMEM(t_pp.shape, BF), in_specs=[an...  73 us
    unnamed x1, local copies, waits for them, and re-layouts  2.02 us
    reduce_sum x1, other arithmetic, slot_values(): jnp.sum(jnp.where(hit, v[None, :], jnp.float32(0.0)), axis=1)  1.93 us

profile of v5, /device:TPU:1, one launch (start us, length us, event | category | flops | bytes accessed | tf_op | source)
XLA Modules:
  0.0 79.3 jit_solution(9763459707386050885)
XLA Ops:
  0.0 0.7 dynamic-slice_convert_fusion
  0.7 0.7 dynamic_slice.7
  1.4 1.9 %select_reduce_fusion.1 = (f32[1024]{0:T(1024)S(1)}, f32[1024]{0:T(1024)S(1)}) fusion(f32[1024]{0:T(1024)S(1)} %dynamic-slice_convert_fusion, s32[1024]{0:T(1024)} %param.9, f32[1024]{0:T(1024)S(1)} %dynamic_slice.7), kind=kLoop, calls=%fused_computation.1 | loop fusion | flops 5240832 | bytes 20480 | tf_op jit(solution)/shard_map/reduce_sum | solution.py:317
  3.3 0.1 stack.9
  3.4 0.1 stack.10
  3.6 0.1 tile.10
  3.7 0.6 broadcast_select_fusion.meta_hbm
  4.3 73.0 %shard_map.64 = bf16[1024,2048]{1,0:T(8,128)(2,1)S(1)} custom-call(bf16[1024,2048]{1,0:T(8,128)(2,1)} %t_hbm.1, bf16[4,4,4,128,512]{4,3,2,1,0:T(8,128)(2,1)} %bitcast.4, f32[4,4,2,2,128]{4,3,2,1,0:T(2,128)} %broadcast_select_fusion.meta_hbm, s32[8,128]{1,0:T(8,128)} %bitcast.5), custom_call_target="tpu_custom_call" | custom-call | tf_op jit(solution)/shard_map/pallas_call | solution.py:331
  77.3 2.0 %copy.8 = bf16[1024,2048]{1,0:T(8,128)(2,1)} copy(bf16[1024,2048]{1,0:T(8,128)(2,1)S(1)} %shard_map.64) | data formatting | bytes 8388608
  (3 shorter events, 0.1 us)

commit v6 on v5

--- a/solution.py
+++ b/solution.py
@@ -7,7 +7,7 @@
 
 NX, NY, NCORE, NZ = 4, 4, 2, 4
 G, GK, NB = 8, 4, 256
-LEAD, LC, LD, PURE, PURE_IN = 4, 2, 5, 5, 13
+LEAD, LC, LD, PURE, PURE_IN = 4, 2, 5, 4, 12
 KINDS = 7
 MESH = pl.DeviceIdType.MESH
 BF = jnp.bfloat16

time: 79.9 us -> 79.9 us (level)
  no operation moved by 1% of the time
where the time goes in v6:
time: 79.9 us; the launch traced here: 79.3 us
  Pallas kernels  72.9 us (91%)
  other arithmetic  3.3 us (4%)
  local copies, waits for them, and re-layouts  3.03 us (4%)
    pallas_call x1, Pallas kernels, on_device(): pl.pallas_call(kernel, out_shape=pltpu.VMEM(t_pp.shape, BF), in_specs=[an...  72.9 us
    unnamed x1, local copies, waits for them, and re-layouts  2.02 us
    reduce_sum x1, other arithmetic, slot_values(): jnp.sum(jnp.where(hit, v[None, :], jnp.float32(0.0)), axis=1)  1.93 us

profile of v6, /device:TPU:1, one launch (start us, length us, event | category | flops | bytes accessed | tf_op | source)
XLA Modules:
  0.0 79.3 jit_solution(7651640789855961058)
XLA Ops:
  0.0 0.7 dynamic-slice_convert_fusion
  0.7 0.7 dynamic_slice.7
  1.4 1.9 %select_reduce_fusion.1 = (f32[1024]{0:T(1024)S(1)}, f32[1024]{0:T(1024)S(1)}) fusion(f32[1024]{0:T(1024)S(1)} %dynamic-slice_convert_fusion, s32[1024]{0:T(1024)} %param.9, f32[1024]{0:T(1024)S(1)} %dynamic_slice.7), kind=kLoop, calls=%fused_computation.1 | loop fusion | flops 5240832 | bytes 20480 | tf_op jit(solution)/shard_map/reduce_sum | solution.py:317
  3.3 0.1 stack.9
  3.4 0.1 stack.10
  3.6 0.1 tile.10
  3.7 0.6 broadcast_select_fusion.meta_hbm
  4.3 72.9 %shard_map.64 = bf16[1024,2048]{1,0:T(8,128)(2,1)S(1)} custom-call(bf16[1024,2048]{1,0:T(8,128)(2,1)} %t_hbm.1, bf16[4,4,4,128,512]{4,3,2,1,0:T(8,128)(2,1)} %bitcast.4, f32[4,4,2,2,128]{4,3,2,1,0:T(2,128)} %broadcast_select_fusion.meta_hbm, s32[8,128]{1,0:T(8,128)} %bitcast.5), custom_call_target="tpu_custom_call" | custom-call | tf_op jit(solution)/shard_map/pallas_call | solution.py:331
  77.3 2.0 %copy.8 = bf16[1024,2048]{1,0:T(8,128)(2,1)} copy(bf16[1024,2048]{1,0:T(8,128)(2,1)S(1)} %shard_map.64) | data formatting | bytes 8388608
  (3 shorter events, 0.1 us)
